TPU v7x, 256 devices: a whole 4x4x8 slice. The times are simulated.
256 devices in a mesh: rows: 64 (over y, z, core), cols: 4 (over x).
Axes of the slice: x: 4, y: 4, z: 8, core: 2. Of those that a mesh axis runs over, the one named last changes fastest.
Arguments:
- residual_block: float32 [524288, 64], P('rows', 'cols'), may hold values from -6 to 6
- basis: bfloat16 [524288, 64], P('rows', 'cols'), may hold values from -0.0078125 to 0.0078125
- fine_tiles: bfloat16 [4096, 4, 128, 128], P('rows')
- fine_index: int32 [4096, 4], P('rows'), may hold values from 0 to 4095, as said below
- mid_tiles: bfloat16 [512, 3, 128, 128], P('rows')
- fine_owner: int32 [524288], P('rows'), may hold values from 0 to 65535, as said below
- mid_owner: int32 [65536], P('rows'), may hold values from 0 to 8191, as said below
- coarse_inverse: float32 [8192, 8192], P('rows'), as said below
Outputs:
- directions: float32 [524288, 64], P('rows', 'cols')
- gram: float32 [64, 64], P(None, 'cols')
Inputs may be any that keep to these rules, and one draw needn't show every extreme that they name: `fine_index`: slot 0 of block row g names g itself; every block named in a block row of partition p (block rows p*64 to p*64 + 63) belongs to partition p - 1, p or p + 1. `fine_owner`: the fine vertices of partition p map to level-one rows p*1024 to p*1024 + 1023; every level-one row receives exactly 8 vertices. `mid_owner`: the level-one rows of partitions 2q and 2q + 1 map to level-two rows 2q*128 to 2q*128 + 2*128 - 1; every level-two row receives exactly 8 level-one rows. coarse_inverse is symmetric.
All inputs are finite; a program needn't handle non-finite values.
Results may differ from a plain program's by a relative error of at most 0.013.
Values may be sent and summed in bfloat16 or wider, within the bound.
A program may use at most 64 MiB of HBM per device.

v0:
```python
import jax
import jax.numpy as jnp
from jax import lax
from jax.sharding import PartitionSpec as P

DAMPING = 0.6666666666666666


def with_halo(array, sides, width):
    for axis, dim in sides:
        peers, length = (lax.axis_size(axis), array.shape[dim])
        up = [(i, (i + 1) % peers) for i in range(peers - 1)]
        down = [(j, i) for i, j in up]
        last = lax.slice_in_dim(array, length - width, length, axis=dim)
        leading = lax.slice_in_dim(array, 0, width, axis=dim)
        before = lax.ppermute(last, axis, up)
        after = lax.ppermute(leading, axis, down)
        array = jnp.concatenate([before, array, after], axis=dim)
    return array


def swapped(value, axis, apart):
    mask = 2**apart
    pairs = [(source, source ^ mask) for source in range(lax.axis_size(axis))]
    return lax.ppermute(value, axis, pairs)


def fine_apply(vector, matrix, window_index):
    extent = matrix.shape[2]
    packed = vector.astype(jnp.bfloat16).reshape(-1, extent, vector.shape[1])
    window = with_halo(packed, (("rows", 0),), packed.shape[0])
    picked = window[window_index]
    product = jnp.einsum("bkij,bkjc->bic", matrix, picked, preferred_element_type=jnp.float32)
    return product.reshape(vector.shape)


def mid_apply(vector, matrix):
    blocks = matrix.shape[0]
    extent = matrix.shape[2]
    packed = vector.astype(jnp.bfloat16).reshape(blocks, extent, vector.shape[1])
    window = with_halo(packed, (("rows", 0),), 1)
    product = jnp.einsum(
        "bij,bjc->bic", matrix[:, 0], window[:-2], preferred_element_type=jnp.float32
    )
    product = product + jnp.einsum(
        "bij,bjc->bic", matrix[:, 1], window[1:-1], preferred_element_type=jnp.float32
    )
    product = product + jnp.einsum(
        "bij,bjc->bic", matrix[:, 2], window[2:], preferred_element_type=jnp.float32
    )
    return product.reshape(vector.shape)


def on_device(
    residual_block, basis, fine_tiles, fine_index, mid_tiles, fine_owner, mid_owner, coarse_inverse
):
    device = lax.axis_index("rows")
    blocks = fine_tiles.shape[0]
    mid_count = mid_tiles.shape[0] * mid_tiles.shape[2]
    coarse_count = coarse_inverse.shape[0]
    col_width = residual_block.shape[1]
    parity = device % 2
    window_index = fine_index - (device - 1) * blocks
    fine_local = fine_owner - device * mid_count
    mid_local = mid_owner - (device - parity) * coarse_count
    fine_inv = 1.0 / jnp.diagonal(fine_tiles[:, 0], axis1=1, axis2=2).astype(jnp.float32).reshape(
        -1, 1
    )
    mid_inv = 1.0 / jnp.diagonal(mid_tiles[:, 1], axis1=1, axis2=2).astype(jnp.float32).reshape(
        -1, 1
    )
    fine_x = DAMPING * fine_inv * residual_block
    fine_x = fine_x + DAMPING * fine_inv * (
        residual_block - fine_apply(fine_x, fine_tiles, window_index)
    )
    fine_res = residual_block - fine_apply(fine_x, fine_tiles, window_index)
    partial_mid = jax.ops.segment_sum(fine_res, fine_local, num_segments=mid_count)
    mid_x = DAMPING * mid_inv * partial_mid
    mid_x = mid_x + DAMPING * mid_inv * (partial_mid - mid_apply(mid_x, mid_tiles))
    mid_res = partial_mid - mid_apply(mid_x, mid_tiles)
    partial_value = jax.ops.segment_sum(mid_res, mid_local, num_segments=2 * coarse_count)
    halves = partial_value.reshape(2, coarse_count, col_width)
    own_half = jnp.where(parity == 0, halves[0], halves[1])
    other_half = jnp.where(parity == 0, halves[1], halves[0])
    coarse_rhs = own_half + swapped(other_half, "rows", 0)
    coarse_fix = jnp.dot(
        coarse_inverse,
        lax.all_gather(coarse_rhs, "rows", axis=0, tiled=True),
        precision=lax.Precision.HIGHEST,
        preferred_element_type=jnp.float32,
    )
    partner_fix = swapped(coarse_fix, "rows", 0)
    pair_values = jnp.where(
        parity == 0,
        jnp.concatenate([coarse_fix, partner_fix], axis=0),
        jnp.concatenate([partner_fix, coarse_fix], axis=0),
    )
    mid_x = mid_x + pair_values[mid_local]
    mid_x = mid_x + DAMPING * mid_inv * (partial_mid - mid_apply(mid_x, mid_tiles))
    fine_x = fine_x + mid_x[fine_local]
    finished = fine_x + DAMPING * fine_inv * (
        residual_block - fine_apply(fine_x, fine_tiles, window_index)
    )
    rounded = finished.astype(jnp.bfloat16)
    partial_gram = lax.dot_general(
        lax.all_gather(basis, "cols", axis=1, tiled=True),
        rounded,
        (((0,), (0,)), ((), ())),
        preferred_element_type=jnp.float32,
    )
    gram = lax.psum(partial_gram, "rows")
    return (finished, gram)


def solution(mesh):
    in_specs = (
        P("rows", "cols"),
        P("rows", "cols"),
        P("rows", None, None, None),
        P("rows", None),
        P("rows", None, None, None),
        P("rows"),
        P("rows"),
        P("rows", None),
    )
    out_specs = (P("rows", "cols"), P(None, "cols"))
    return jax.shard_map(
        on_device, mesh=mesh, in_specs=in_specs, out_specs=out_specs, check_vma=False
    )
```

profile of v0, /device:TPU:4, one launch (start us, length us, event | category | flops | bytes accessed | tf_op | source)
XLA Modules:
  0.0 407.9 jit_solution(2754003155523653004)
XLA Ops:
  8.8 3.9 copy.204
  12.7 1.9 gather_fusion
  19.1 3.1 copy.166
  25.2 5.7 %convolution_bitcast_fusion.2 = f32[64,2,8,128]{3,2,1,0:T(8,128)S(1)} fusion(bf16[64,4,128,16]{2,3,1,0:T(8,128)(2,1)S(1)} %bitcast.177, bf16[64,4,128,128]{3,2,1,0:T(8,128)(2,1)} %param.10), kind=kOutput, calls=%fused_computation.11 | convolution fusion | flops 134217728 | bytes 9961472 | tf_op jit(solution)/shard_map/bkij,bkjc->bic/dot_general | solution.py:33
  31.0 4.7 %collective-permute-start.2 = (bf16[64,128,16]{1,2,0:T(8,128)(2,1)S(1)}, bf16[64,128,16]{1,2,0:T(8,128)(2,1)S(1)}, u32[]{:S(2)}, u32[]{:S(2)}) collective-permute-start(bf16[64,128,16]{1,2,0:T(8,128)(2,1)S(1)} %copy_bitcast_fusion.1), channel_id=1, source_target_pairs={{0,4},{4,8},{8,12},{12,16},{16,20},{20,24},{24,28},{28,32},{32,36}... | collective-permute-start | bytes 786440 | tf_op jit(solution)/shard_map/ppermute | solution.py:16
  37.1 3.3 collective-permute-done.3
  41.3 5.7 %convolution_bitcast_fusion.1 = f32[64,2,8,128]{3,2,1,0:T(8,128)S(1)} fusion(bf16[64,4,128,16]{2,3,1,0:T(8,128)(2,1)S(1)} %bitcast.178, bf16[64,4,128,128]{3,2,1,0:T(8,128)(2,1)} %param.10), kind=kOutput, calls=%fused_computation.10 | convolution fusion | flops 134217728 | bytes 9961472 | tf_op jit(solution)/shard_map/bkij,bkjc->bic/dot_general | solution.py:33
  47.1 2.6 copy.172
  49.7 44.4 %scatter_custom_fusion = f32[1024,16]{1,0:T(8,128)S(1)} fusion(s32[8192]{0:T(1024)S(1)} %get-tuple-element.11, f32[8192,16]{1,0:T(8,128)} %copy.172, f32[]{:T(128)} %constant.25.clone.1), kind=kCustom, calls=%fused_computation.51 | custom fusion | flops 131072 | bytes 66048 | tf_op jit(solution)/shard_map/scatter-add | solution.py:77
  95.9 7.3 %collective-permute-start.4 = (bf16[1,128,16]{1,2,0:T(8,128)(2,1)S(1)}, bf16[1,128,16]{1,2,0:T(8,128)(2,1)S(1)}, u32[]{:S(2)}, u32[]{:S(2)}) collective-permute-start(bf16[1,128,16]{1,2,0:T(8,128)(2,1)S(1)} %get-tuple-element.18), channel_id=1, source_target_pairs={{0,4},{4,8},{8,12},{12,16},{16,20},{20,24},{24,28},{28,32},{32,36}... | collective-permute-start | bytes 12296 | tf_op jit(solution)/shard_map/ppermute | solution.py:16
  105.8 4.2 %collective-permute-start.6 = (bf16[1,128,16]{1,2,0:T(8,128)(2,1)S(1)}, bf16[1,128,16]{1,2,0:T(8,128)(2,1)S(1)}, u32[]{:S(2)}, u32[]{:S(2)}) collective-permute-start(bf16[1,128,16]{1,2,0:T(8,128)(2,1)S(1)} %get-tuple-element.16), channel_id=1, source_target_pairs={{0,4},{4,8},{8,12},{12,16},{16,20},{20,24},{24,28},{28,32},{32,36}... | collective-permute-start | bytes 12296 | tf_op jit(solution)/shard_map/ppermute | solution.py:16
  112.2 6.4 %scatter_custom_fusion.1 = f32[256,16]{1,0:T(8,128)S(1)} fusion(s32[1024]{0:T(1024)S(1)} %get-tuple-element.13, f32[1024,16]{1,0:T(8,128)} %bitcast_subtract_fusion.3, f32[]{:T(128)} %constant.25.clone.1), kind=kCustom, calls=%fused_computation.70 | custom fusion | flops 16384 | bytes 16896 | tf_op jit(solution)/shard_map/scatter-add | solution.py:81
  118.6 2.5 collective-permute-start.8
  122.0 65.2 %all_gather.6 = f32[8192,16]{1,0:T(8,128)S(1)} all-gather(f32[128,16]{1,0:T(8,128)S(1)} %select_add_fusion), channel_id=1, replica_groups=mesh['rows'=64,'cols'=4] {'rows'}, dimensions={0}, use_global_device_ids=true | all-gather | bytes 532480 | tf_op jit(solution)/shard_map/all_gather | solution.py:88
  187.2 6.6 %convolution_bitcast_fusion.4 = f32[128,16]{0,1:T(8,128)S(1)} fusion(f32[8192,16]{1,0:T(8,128)S(1)} %all_gather.6, f32[128,8192]{1,0:T(8,128)S(1)} %copy-done.2), kind=kOutput, calls=%fused_computation.22 | convolution fusion | flops 201326592 | bytes 4726784 | tf_op jit(solution)/shard_map/dot_general | solution.py:86
  195.1 2.8 gather_fusion.4
  199.7 3.0 collective-permute-start.10
  204.0 27.9 %gather_fusion.5 = f32[8192,16]{1,0:T(8,128)} fusion(f32[1024,16]{1,0:T(8,128)S(1)} %copy.193, s32[8192]{0:T(1024)S(1)} %get-tuple-element.10), kind=kCustom, calls=%fused_computation.5 | custom fusion | bytes 1081344 | tf_op jit(solution)/shard_map/gather | solution.py:100
  231.9 2.8 copy.194
  234.8 3.4 collective-permute-start.12
  239.6 3.9 collective-permute-done.13
  244.4 5.7 %convolution_bitcast_fusion = f32[64,2,8,128]{3,2,1,0:T(8,128)S(1)} fusion(bf16[64,4,128,16]{2,3,1,0:T(8,128)(2,1)S(1)} %bitcast.176, bf16[64,4,128,128]{3,2,1,0:T(8,128)(2,1)} %param.10), kind=kOutput, calls=%fused_computation.9 | convolution fusion | flops 134217728 | bytes 9961472 | tf_op jit(solution)/shard_map/bkij,bkjc->bic/dot_general | solution.py:33
  250.3 18.4 %all-gather.2.cloned.1.call-done = bf16[8192,64]{0,1:T(8,128)(2,1)} async-done(((bf16[8192,16]{0,1:T(8,128)(2,1)}), bf16[8192,64]{0,1:T(8,128)(2,1)}) %all-gather.2.cloned.1.call-update) | async-done | bytes 1048592 | tf_op jit(solution)/shard_map/all_gather | solution.py:106
  270.3 130.8 %psum.7 = f32[64,16]{0,1:T(8,128)} all-reduce(f32[64,16]{0,1:T(8,128)S(1)} %convolution_bitcast_fusion.3), channel_id=1, replica_groups=mesh['rows'=64,'cols'=4] {'rows'}, use_global_device_ids=true, to_apply=%region_2.3 | all-reduce | flops 1024 | bytes 8192 | tf_op jit(solution)/shard_map/psum | solution.py:111
  (91 shorter events, 27.2 us)
Async XLA Ops:
  7.2 1.6 slice-start
  7.2 261.5 %all-gather.2.cloned.1.call-start = ((), (), s32[]{:S(2)}) async-start(), calls=%async_computation | async-start | bytes 1310720 | tf_op jit(solution)/shard_map/all_gather | solution.py:106
  8.8 6.0 %copy-start = (f32[8192,16]{0,1:T(8,128)S(1)}, f32[8192,16]{0,1:T(8,128)}, u32[]{:S(2)}) copy-start(f32[8192,16]{0,1:T(8,128)} %param.8) | copy-start | bytes 1572868
  8.8 9.1 %copy-start.6 = (s32[64,4]{0,1:T(4,128)S(1)}, s32[64,4]{0,1:T(4,128)}, u32[]{:S(2)}) copy-start(s32[64,4]{0,1:T(4,128)} %param.11) | copy-start | bytes 3076
  12.7 11.5 %copy-start.5 = (s32[1024]{0:T(1024)S(1)}, s32[1024]{0:T(1024)}, u32[]{:S(2)}) copy-start(s32[1024]{0:T(1024)} %param.14) | copy-start | bytes 12292
  14.8 9.4 %collective-permute-start = (bf16[64,128,16]{1,2,0:T(8,128)(2,1)S(1)}, bf16[64,128,16]{1,2,0:T(8,128)(2,1)S(1)}, u32[]{:S(2)}, u32[]{:S(2)}) collective-permute-start(bf16[64,128,16]{1,2,0:T(8,128)(2,1)S(1)} %copy_bitcast_fusion.2), channel_id=1, source_target_pairs={{0,4},{4,8},{8,12},{12,16},{16,20},{20,24},{24,28},{28,32},{32,36}... | collective-permute-start | bytes 786440 | tf_op jit(solution)/shard_map/ppermute | solution.py:16
  16.5 7.7 %collective-permute-start.1 = (bf16[64,128,16]{1,2,0:T(8,128)(2,1)S(1)}, bf16[64,128,16]{1,2,0:T(8,128)(2,1)S(1)}, u32[]{:S(2)}, u32[]{:S(2)}) collective-permute-start(bf16[64,128,16]{1,2,0:T(8,128)(2,1)S(1)} %copy_bitcast_fusion.2), channel_id=1, source_target_pairs={{4,0},{8,4},{12,8},{16,12},{20,16},{24,20},{28,24},{32,28},{36,32}... | collective-permute-start | bytes 786440 | tf_op jit(solution)/shard_map/ppermute | solution.py:17
  25.2 11.9 %copy-start.4 = (s32[8192]{0:T(1024)S(1)}, s32[8192]{0:T(1024)}, u32[]{:S(2)}) copy-start(s32[8192]{0:T(1024)} %param.13) | copy-start | bytes 98308
  31.0 6.1 %collective-permute-start.2 = (bf16[64,128,16]{1,2,0:T(8,128)(2,1)S(1)}, bf16[64,128,16]{1,2,0:T(8,128)(2,1)S(1)}, u32[]{:S(2)}, u32[]{:S(2)}) collective-permute-start(bf16[64,128,16]{1,2,0:T(8,128)(2,1)S(1)} %copy_bitcast_fusion.1), channel_id=1, source_target_pairs={{0,4},{4,8},{8,12},{12,16},{16,20},{20,24},{24,28},{28,32},{32,36}... | collective-permute-start | bytes 786440 | tf_op jit(solution)/shard_map/ppermute | solution.py:16
  35.7 4.7 %collective-permute-start.3 = (bf16[64,128,16]{1,2,0:T(8,128)(2,1)S(1)}, bf16[64,128,16]{1,2,0:T(8,128)(2,1)S(1)}, u32[]{:S(2)}, u32[]{:S(2)}) collective-permute-start(bf16[64,128,16]{1,2,0:T(8,128)(2,1)S(1)} %copy_bitcast_fusion.1), channel_id=1, source_target_pairs={{4,0},{8,4},{12,8},{16,12},{20,16},{24,20},{28,24},{32,28},{36,32}... | collective-permute-start | bytes 786440 | tf_op jit(solution)/shard_map/ppermute | solution.py:17
  47.0 47.3 %copy-start.1 = (bf16[8,3,128,128]{3,2,1,0:T(8,128)(2,1)S(1)}, bf16[8,3,128,128]{3,2,1,0:T(8,128)(2,1)}, u32[]{:S(2)}) copy-start(bf16[8,3,128,128]{3,2,1,0:T(8,128)(2,1)} %param.12) | copy-start | bytes 2359300
  94.6 8.6 %collective-permute-start.5 = (bf16[1,128,16]{1,2,0:T(8,128)(2,1)S(1)}, bf16[1,128,16]{1,2,0:T(8,128)(2,1)S(1)}, u32[]{:S(2)}, u32[]{:S(2)}) collective-permute-start(bf16[1,128,16]{1,2,0:T(8,128)(2,1)S(1)} %get-tuple-element.19), channel_id=1, source_target_pairs={{4,0},{8,4},{12,8},{16,12},{20,16},{24,20},{28,24},{32,28},{36,32}... | collective-permute-start | bytes 12296 | tf_op jit(solution)/shard_map/ppermute | solution.py:17
  95.9 8.1 %collective-permute-start.4 = (bf16[1,128,16]{1,2,0:T(8,128)(2,1)S(1)}, bf16[1,128,16]{1,2,0:T(8,128)(2,1)S(1)}, u32[]{:S(2)}, u32[]{:S(2)}) collective-permute-start(bf16[1,128,16]{1,2,0:T(8,128)(2,1)S(1)} %get-tuple-element.18), channel_id=1, source_target_pairs={{0,4},{4,8},{8,12},{12,16},{16,20},{20,24},{24,28},{28,32},{32,36}... | collective-permute-start | bytes 12296 | tf_op jit(solution)/shard_map/ppermute | solution.py:16
  104.5 5.5 %collective-permute-start.7 = (bf16[1,128,16]{1,2,0:T(8,128)(2,1)S(1)}, bf16[1,128,16]{1,2,0:T(8,128)(2,1)S(1)}, u32[]{:S(2)}, u32[]{:S(2)}) collective-permute-start(bf16[1,128,16]{1,2,0:T(8,128)(2,1)S(1)} %get-tuple-element.17), channel_id=1, source_target_pairs={{4,0},{8,4},{12,8},{16,12},{20,16},{24,20},{28,24},{32,28},{36,32}... | collective-permute-start | bytes 12296 | tf_op jit(solution)/shard_map/ppermute | solution.py:17
  105.8 5.0 %collective-permute-start.6 = (bf16[1,128,16]{1,2,0:T(8,128)(2,1)S(1)}, bf16[1,128,16]{1,2,0:T(8,128)(2,1)S(1)}, u32[]{:S(2)}, u32[]{:S(2)}) collective-permute-start(bf16[1,128,16]{1,2,0:T(8,128)(2,1)S(1)} %get-tuple-element.16), channel_id=1, source_target_pairs={{0,4},{4,8},{8,12},{12,16},{16,20},{20,24},{24,28},{28,32},{32,36}... | collective-permute-start | bytes 12296 | tf_op jit(solution)/shard_map/ppermute | solution.py:16
  118.6 68.6 %copy-start.2 = (f32[128,8192]{1,0:T(8,128)S(1)}, f32[128,8192]{1,0:T(8,128)}, u32[]{:S(2)}) copy-start(f32[128,8192]{1,0:T(8,128)} %param.15) | copy-start | bytes 12582916
  118.6 3.4 collective-permute-start.8
  193.8 1.2 collective-permute-start.9
  198.4 4.4 %collective-permute-start.11 = (bf16[1,128,16]{1,2,0:T(8,128)(2,1)S(1)}, bf16[1,128,16]{1,2,0:T(8,128)(2,1)S(1)}, u32[]{:S(2)}, u32[]{:S(2)}) collective-permute-start(bf16[1,128,16]{1,2,0:T(8,128)(2,1)S(1)} %get-tuple-element.15), channel_id=1, source_target_pairs={{4,0},{8,4},{12,8},{16,12},{20,16},{24,20},{28,24},{32,28},{36,32}... | collective-permute-start | bytes 12296 | tf_op jit(solution)/shard_map/ppermute | solution.py:17
  199.7 3.8 collective-permute-start.10
  234.8 4.8 %collective-permute-start.12 = (bf16[64,128,16]{1,2,0:T(8,128)(2,1)S(1)}, bf16[64,128,16]{1,2,0:T(8,128)(2,1)S(1)}, u32[]{:S(2)}, u32[]{:S(2)}) collective-permute-start(bf16[64,128,16]{1,2,0:T(8,128)(2,1)S(1)} %copy_bitcast_fusion), channel_id=1, source_target_pairs={{0,4},{4,8},{8,12},{12,16},{16,20},{20,24},{24,28},{28,32},{32,36}... | collective-permute-start | bytes 786440 | tf_op jit(solution)/shard_map/ppermute | solution.py:16
  238.3 5.2 %collective-permute-start.13 = (bf16[64,128,16]{1,2,0:T(8,128)(2,1)S(1)}, bf16[64,128,16]{1,2,0:T(8,128)(2,1)S(1)}, u32[]{:S(2)}, u32[]{:S(2)}) collective-permute-start(bf16[64,128,16]{1,2,0:T(8,128)(2,1)S(1)} %copy_bitcast_fusion), channel_id=1, source_target_pairs={{4,0},{8,4},{12,8},{16,12},{20,16},{24,20},{28,24},{32,28},{36,32}... | collective-permute-start | bytes 786440 | tf_op jit(solution)/shard_map/ppermute | solution.py:17
  250.3 150.8 %copy-start.3 = (f32[8192,16]{0,1:T(8,128)}, f32[8192,16]{0,1:T(8,128)S(1)}, u32[]{:S(2)}) copy-start(f32[8192,16]{0,1:T(8,128)S(1)} %fusion.7) | copy-start | bytes 1572868
Sparse Core Ops, SparseCore 0:
  239.7 28.9 all-gather.1
where the time goes:
time: 409 us; the launch traced here: 408 us
  blocking collectives  196 us (48%)
  local copies, waits for them, and re-layouts  53.3 us (13%)
  other arithmetic  52.8 us (13%)
  starting transfers between devices  35.1 us (9%)
  waiting for transfers between devices  29 us (7%)
  matrix products  27.3 us (7%)
  between operations  14.5 us (4%)
    psum x1, blocking collectives, on_device(): gram = lax.psum(partial_gram, 'rows')  131 us
    all_gather x1, blocking collectives, on_device(): lax.all_gather(coarse_rhs, 'rows', axis=0, tiled=True)  65.2 us
    scatter-add x1, other arithmetic, on_device(): jax.ops.segment_sum(fine_res, fine_local, num_segments=mid_count)  44.4 us
    gather x2, local copies, waits for them, and re-layouts, on_device(): fine_x = fine_x + mid_x[fine_local]  30.7 us
    ppermute x6, starting transfers between devices, with_halo(): before = lax.ppermute(last, axis, up)  24.4 us
    all_gather x1, waiting for transfers between devices, on_device(): lax.all_gather(basis, 'cols', axis=1, tiled=True)  18.4 us
    dot_general x3, matrix products, fine_apply(): jnp.einsum('bkij,bkjc->bic', matrix, picked, preferred_element_type=jnp.f...  17 us
  transfers between devices with their start and end apart: 15, of which 8 were waited for; matrix products, arithmetic and copies ran while one was open for 3% of the time, Pallas kernels for 0%

commit v1 on v0

--- a/solution.py
+++ b/solution.py
@@ -103,7 +103,9 @@
     )
     rounded = finished.astype(jnp.bfloat16)
     partial_gram = lax.dot_general(
-        lax.all_gather(basis, "cols", axis=1, tiled=True),
+        jnp.concatenate(
+            lax.all_to_all(jnp.stack(lax.axis_size("cols") * [basis], 0), "cols", 0, 0), 1
+        ),
         rounded,
         (((0,), (0,)), ((), ())),
         preferred_element_type=jnp.float32,

time: 409 us -> 383 us (0.936)
  waiting for transfers between devices: 29 us -> 10.9 us
  between operations: 14.5 us -> 1.13 us
  starting transfers between devices: 35.1 us -> 39.8 us
    all_gather x1 -> x0, waiting for transfers between devices: 18.4 us -> none  [on_device(): lax.all_gather(basis, 'cols', axis=1, tiled=True)]
    all_to_all x0 -> x1, starting transfers between devices: none -> 4.8 us  [on_device(): lax.all_to_all(jnp.stack(lax.axis_size('cols') * [basis], 0), 'cols', 0, 0)]
    all_to_all x0 -> x1, waiting for transfers between devices: none -> 4.17 us  [on_device(): lax.all_to_all(jnp.stack(lax.axis_size('cols') * [basis], 0), 'cols', 0, 0)]
  transfers between devices with their start and end apart: 15 -> 15, of which waited for: 8 -> 7; matrix products, arithmetic and copies ran while one was open for 3% -> 4% of each run, Pallas kernels for 0% -> 0%
where the time goes in v1:
time: 383 us; the launch traced here: 381 us
  blocking collectives  195 us (51%)
  local copies, waits for them, and re-layouts  54.4 us (14%)
  other arithmetic  52.8 us (14%)
  starting transfers between devices  39.8 us (10%)
  matrix products  27.3 us (7%)
  waiting for transfers between devices  10.9 us (3%)
    psum x1, blocking collectives, on_device(): gram = lax.psum(partial_gram, 'rows')  130 us
    all_gather x1, blocking collectives, on_device(): lax.all_gather(coarse_rhs, 'rows', axis=0, tiled=True)  65.2 us
    scatter-add x1, other arithmetic, on_device(): jax.ops.segment_sum(fine_res, fine_local, num_segments=mid_count)  44.4 us
    gather x2, local copies, waits for them, and re-layouts, on_device(): fine_x = fine_x + mid_x[fine_local]  30.7 us
    ppermute x6, starting transfers between devices, with_halo(): before = lax.ppermute(last, axis, up)  24.4 us
    dot_general x3, matrix products, fine_apply(): jnp.einsum('bkij,bkjc->bic', matrix, picked, preferred_element_type=jnp.f...  17 us
    ppermute x6, starting transfers between devices, with_halo(): after = lax.ppermute(leading, axis, down)  7.78 us
  transfers between devices with their start and end apart: 15, of which 7 were waited for; matrix products, arithmetic and copies ran while one was open for 4% of the time, Pallas kernels for 0%

profile of v1, /device:TPU:4, one launch (start us, length us, event | category | flops | bytes accessed | tf_op | source)
XLA Modules:
  0.0 381.3 jit_solution(17093240672775462713)
XLA Ops:
  2.2 3.9 %copy.205 = bf16[64,1,128,128]{0,3,2,1:T(8,128)(2,1)} copy(bf16[64,1,128,128]{3,2,1,0:T(8,128)(2,1)S(1)} %slice-done) | data formatting | bytes 4194304
  6.1 1.9 gather_fusion
  12.5 3.1 copy.167
  18.7 5.7 %convolution_bitcast_fusion.2 = f32[64,2,8,128]{3,2,1,0:T(8,128)S(1)} fusion(bf16[64,4,128,16]{2,3,1,0:T(8,128)(2,1)S(1)} %bitcast.180, bf16[64,4,128,128]{3,2,1,0:T(8,128)(2,1)} %param.10), kind=kOutput, calls=%fused_computation.11 | convolution fusion | flops 134217728 | bytes 9961472 | tf_op jit(solution)/shard_map/bkij,bkjc->bic/dot_general | solution.py:33
  24.5 4.7 %collective-permute-start.2 = (bf16[64,128,16]{1,2,0:T(8,128)(2,1)S(1)}, bf16[64,128,16]{1,2,0:T(8,128)(2,1)S(1)}, u32[]{:S(2)}, u32[]{:S(2)}) collective-permute-start(bf16[64,128,16]{1,2,0:T(8,128)(2,1)S(1)} %copy_bitcast_fusion.1), channel_id=1, source_target_pairs={{0,4},{4,8},{8,12},{12,16},{16,20},{20,24},{24,28},{28,32},{32,36}... | collective-permute-start | bytes 786440 | tf_op jit(solution)/shard_map/ppermute | solution.py:16
  30.6 3.3 collective-permute-done.3
  34.8 5.7 %convolution_bitcast_fusion.1 = f32[64,2,8,128]{3,2,1,0:T(8,128)S(1)} fusion(bf16[64,4,128,16]{2,3,1,0:T(8,128)(2,1)S(1)} %bitcast.181, bf16[64,4,128,128]{3,2,1,0:T(8,128)(2,1)} %param.10), kind=kOutput, calls=%fused_computation.10 | convolution fusion | flops 134217728 | bytes 9961472 | tf_op jit(solution)/shard_map/bkij,bkjc->bic/dot_general | solution.py:33
  40.5 2.6 copy.173
  43.2 44.4 %scatter_custom_fusion = f32[1024,16]{1,0:T(8,128)S(1)} fusion(s32[8192]{0:T(1024)S(1)} %get-tuple-element.11, f32[8192,16]{1,0:T(8,128)} %copy.173, f32[]{:T(128)} %constant.25.clone.1), kind=kCustom, calls=%fused_computation.51 | custom fusion | flops 131072 | bytes 66048 | tf_op jit(solution)/shard_map/scatter-add | solution.py:77
  89.4 7.3 %collective-permute-start.4 = (bf16[1,128,16]{1,2,0:T(8,128)(2,1)S(1)}, bf16[1,128,16]{1,2,0:T(8,128)(2,1)S(1)}, u32[]{:S(2)}, u32[]{:S(2)}) collective-permute-start(bf16[1,128,16]{1,2,0:T(8,128)(2,1)S(1)} %get-tuple-element.18), channel_id=1, source_target_pairs={{0,4},{4,8},{8,12},{12,16},{16,20},{20,24},{24,28},{28,32},{32,36}... | collective-permute-start | bytes 12296 | tf_op jit(solution)/shard_map/ppermute | solution.py:16
  99.3 4.2 %collective-permute-start.6 = (bf16[1,128,16]{1,2,0:T(8,128)(2,1)S(1)}, bf16[1,128,16]{1,2,0:T(8,128)(2,1)S(1)}, u32[]{:S(2)}, u32[]{:S(2)}) collective-permute-start(bf16[1,128,16]{1,2,0:T(8,128)(2,1)S(1)} %get-tuple-element.16), channel_id=1, source_target_pairs={{0,4},{4,8},{8,12},{12,16},{16,20},{20,24},{24,28},{28,32},{32,36}... | collective-permute-start | bytes 12296 | tf_op jit(solution)/shard_map/ppermute | solution.py:16
  105.6 6.4 %scatter_custom_fusion.1 = f32[256,16]{1,0:T(8,128)S(1)} fusion(s32[1024]{0:T(1024)S(1)} %get-tuple-element.13, f32[1024,16]{1,0:T(8,128)} %bitcast_subtract_fusion.3, f32[]{:T(128)} %constant.25.clone.1), kind=kCustom, calls=%fused_computation.70 | custom fusion | flops 16384 | bytes 16896 | tf_op jit(solution)/shard_map/scatter-add | solution.py:81
  112.1 2.5 collective-permute-start.8
  115.5 65.2 %all_gather.3 = f32[8192,16]{1,0:T(8,128)S(1)} all-gather(f32[128,16]{1,0:T(8,128)S(1)} %select_add_fusion), channel_id=1, replica_groups=mesh['rows'=64,'cols'=4] {'rows'}, dimensions={0}, use_global_device_ids=true | all-gather | bytes 532480 | tf_op jit(solution)/shard_map/all_gather | solution.py:88
  180.7 6.6 %convolution_bitcast_fusion.4 = f32[128,16]{0,1:T(8,128)S(1)} fusion(f32[8192,16]{1,0:T(8,128)S(1)} %all_gather.3, f32[128,8192]{1,0:T(8,128)S(1)} %copy-done.2), kind=kOutput, calls=%fused_computation.22 | convolution fusion | flops 201326592 | bytes 4726784 | tf_op jit(solution)/shard_map/dot_general | solution.py:86
  188.6 2.8 gather_fusion.4
  193.2 3.0 collective-permute-start.10
  197.5 27.9 %gather_fusion.5 = f32[8192,16]{1,0:T(8,128)} fusion(f32[1024,16]{1,0:T(8,128)S(1)} %copy.194, s32[8192]{0:T(1024)S(1)} %get-tuple-element.10), kind=kCustom, calls=%fused_computation.5 | custom fusion | bytes 1081344 | tf_op jit(solution)/shard_map/gather | solution.py:100
  225.4 2.8 copy.195
  228.4 3.4 collective-permute-start.12
  234.1 4.8 %all-to-all-start = ((bf16[4,8192,16]{1,2,0:T(8,128)(2,1)}), bf16[4,8192,16]{1,2,0:T(8,128)(2,1)}, u32[]{:S(2)}, u32[]{:S(2)}) async-start(bf16[4,8192,16]{1,2,0:T(8,128)(2,1)} %stack.2), calls=%async_computation | async-start | bytes 2097152 | tf_op jit(solution)/shard_map/all_to_all | solution.py:107
  239.9 5.7 %convolution_bitcast_fusion = f32[64,2,8,128]{3,2,1,0:T(8,128)S(1)} fusion(bf16[64,4,128,16]{2,3,1,0:T(8,128)(2,1)S(1)} %bitcast.179, bf16[64,4,128,128]{3,2,1,0:T(8,128)(2,1)} %param.10), kind=kOutput, calls=%fused_computation.9 | convolution fusion | flops 134217728 | bytes 9961472 | tf_op jit(solution)/shard_map/bkij,bkjc->bic/dot_general | solution.py:33
  245.8 4.2 %all-to-all-done = bf16[4,8192,16]{1,2,0:T(8,128)(2,1)} async-done(((bf16[4,8192,16]{1,2,0:T(8,128)(2,1)}), bf16[4,8192,16]{1,2,0:T(8,128)(2,1)}, u32[]{:S(2)}, u32[]{:S(2)}) %all-to-all-start) | async-done | bytes 1048608 | tf_op jit(solution)/shard_map/all_to_all | solution.py:107
  251.5 129.7 %psum.7 = f32[64,16]{0,1:T(8,128)} all-reduce(f32[64,16]{0,1:T(8,128)S(1)} %convolution_bitcast_fusion.3), channel_id=1, replica_groups=mesh['rows'=64,'cols'=4] {'rows'}, use_global_device_ids=true, to_apply=%region_2.3 | all-reduce | flops 1024 | bytes 8192 | tf_op jit(solution)/shard_map/psum | solution.py:113
  (93 shorter events, 28.2 us)
Async XLA Ops:
  0.6 1.6 slice-start
  2.2 6.0 %copy-start = (f32[8192,16]{0,1:T(8,128)S(1)}, f32[8192,16]{0,1:T(8,128)}, u32[]{:S(2)}) copy-start(f32[8192,16]{0,1:T(8,128)} %param.8) | copy-start | bytes 1572868
  2.2 9.1 %copy-start.7 = (s32[64,4]{0,1:T(4,128)S(1)}, s32[64,4]{0,1:T(4,128)}, u32[]{:S(2)}) copy-start(s32[64,4]{0,1:T(4,128)} %param.11) | copy-start | bytes 3076
  6.1 11.5 %copy-start.6 = (s32[1024]{0:T(1024)S(1)}, s32[1024]{0:T(1024)}, u32[]{:S(2)}) copy-start(s32[1024]{0:T(1024)} %param.14) | copy-start | bytes 12292
  8.2 9.4 %collective-permute-start = (bf16[64,128,16]{1,2,0:T(8,128)(2,1)S(1)}, bf16[64,128,16]{1,2,0:T(8,128)(2,1)S(1)}, u32[]{:S(2)}, u32[]{:S(2)}) collective-permute-start(bf16[64,128,16]{1,2,0:T(8,128)(2,1)S(1)} %copy_bitcast_fusion.2), channel_id=1, source_target_pairs={{0,4},{4,8},{8,12},{12,16},{16,20},{20,24},{24,28},{28,32},{32,36}... | collective-permute-start | bytes 786440 | tf_op jit(solution)/shard_map/ppermute | solution.py:16
  10.0 7.7 %collective-permute-start.1 = (bf16[64,128,16]{1,2,0:T(8,128)(2,1)S(1)}, bf16[64,128,16]{1,2,0:T(8,128)(2,1)S(1)}, u32[]{:S(2)}, u32[]{:S(2)}) collective-permute-start(bf16[64,128,16]{1,2,0:T(8,128)(2,1)S(1)} %copy_bitcast_fusion.2), channel_id=1, source_target_pairs={{4,0},{8,4},{12,8},{16,12},{20,16},{24,20},{28,24},{32,28},{36,32}... | collective-permute-start | bytes 786440 | tf_op jit(solution)/shard_map/ppermute | solution.py:17
  18.7 11.9 %copy-start.5 = (s32[8192]{0:T(1024)S(1)}, s32[8192]{0:T(1024)}, u32[]{:S(2)}) copy-start(s32[8192]{0:T(1024)} %param.13) | copy-start | bytes 98308
  24.5 6.1 %collective-permute-start.2 = (bf16[64,128,16]{1,2,0:T(8,128)(2,1)S(1)}, bf16[64,128,16]{1,2,0:T(8,128)(2,1)S(1)}, u32[]{:S(2)}, u32[]{:S(2)}) collective-permute-start(bf16[64,128,16]{1,2,0:T(8,128)(2,1)S(1)} %copy_bitcast_fusion.1), channel_id=1, source_target_pairs={{0,4},{4,8},{8,12},{12,16},{16,20},{20,24},{24,28},{28,32},{32,36}... | collective-permute-start | bytes 786440 | tf_op jit(solution)/shard_map/ppermute | solution.py:16
  29.2 4.7 %collective-permute-start.3 = (bf16[64,128,16]{1,2,0:T(8,128)(2,1)S(1)}, bf16[64,128,16]{1,2,0:T(8,128)(2,1)S(1)}, u32[]{:S(2)}, u32[]{:S(2)}) collective-permute-start(bf16[64,128,16]{1,2,0:T(8,128)(2,1)S(1)} %copy_bitcast_fusion.1), channel_id=1, source_target_pairs={{4,0},{8,4},{12,8},{16,12},{20,16},{24,20},{28,24},{32,28},{36,32}... | collective-permute-start | bytes 786440 | tf_op jit(solution)/shard_map/ppermute | solution.py:17
  40.5 47.3 %copy-start.1 = (bf16[8,3,128,128]{3,2,1,0:T(8,128)(2,1)S(1)}, bf16[8,3,128,128]{3,2,1,0:T(8,128)(2,1)}, u32[]{:S(2)}) copy-start(bf16[8,3,128,128]{3,2,1,0:T(8,128)(2,1)} %param.12) | copy-start | bytes 2359300
  88.0 8.6 %collective-permute-start.5 = (bf16[1,128,16]{1,2,0:T(8,128)(2,1)S(1)}, bf16[1,128,16]{1,2,0:T(8,128)(2,1)S(1)}, u32[]{:S(2)}, u32[]{:S(2)}) collective-permute-start(bf16[1,128,16]{1,2,0:T(8,128)(2,1)S(1)} %get-tuple-element.19), channel_id=1, source_target_pairs={{4,0},{8,4},{12,8},{16,12},{20,16},{24,20},{28,24},{32,28},{36,32}... | collective-permute-start | bytes 12296 | tf_op jit(solution)/shard_map/ppermute | solution.py:17
  89.4 8.1 %collective-permute-start.4 = (bf16[1,128,16]{1,2,0:T(8,128)(2,1)S(1)}, bf16[1,128,16]{1,2,0:T(8,128)(2,1)S(1)}, u32[]{:S(2)}, u32[]{:S(2)}) collective-permute-start(bf16[1,128,16]{1,2,0:T(8,128)(2,1)S(1)} %get-tuple-element.18), channel_id=1, source_target_pairs={{0,4},{4,8},{8,12},{12,16},{16,20},{20,24},{24,28},{28,32},{32,36}... | collective-permute-start | bytes 12296 | tf_op jit(solution)/shard_map/ppermute | solution.py:16
  98.0 5.5 %collective-permute-start.7 = (bf16[1,128,16]{1,2,0:T(8,128)(2,1)S(1)}, bf16[1,128,16]{1,2,0:T(8,128)(2,1)S(1)}, u32[]{:S(2)}, u32[]{:S(2)}) collective-permute-start(bf16[1,128,16]{1,2,0:T(8,128)(2,1)S(1)} %get-tuple-element.17), channel_id=1, source_target_pairs={{4,0},{8,4},{12,8},{16,12},{20,16},{24,20},{28,24},{32,28},{36,32}... | collective-permute-start | bytes 12296 | tf_op jit(solution)/shard_map/ppermute | solution.py:17
  99.3 5.0 %collective-permute-start.6 = (bf16[1,128,16]{1,2,0:T(8,128)(2,1)S(1)}, bf16[1,128,16]{1,2,0:T(8,128)(2,1)S(1)}, u32[]{:S(2)}, u32[]{:S(2)}) collective-permute-start(bf16[1,128,16]{1,2,0:T(8,128)(2,1)S(1)} %get-tuple-element.16), channel_id=1, source_target_pairs={{0,4},{4,8},{8,12},{12,16},{16,20},{20,24},{24,28},{28,32},{32,36}... | collective-permute-start | bytes 12296 | tf_op jit(solution)/shard_map/ppermute | solution.py:16
  112.1 68.6 %copy-start.2 = (f32[128,8192]{1,0:T(8,128)S(1)}, f32[128,8192]{1,0:T(8,128)}, u32[]{:S(2)}) copy-start(f32[128,8192]{1,0:T(8,128)} %param.15) | copy-start | bytes 12582916
  112.1 3.4 collective-permute-start.8
  187.3 1.2 collective-permute-start.9
  191.9 4.4 %collective-permute-start.11 = (bf16[1,128,16]{1,2,0:T(8,128)(2,1)S(1)}, bf16[1,128,16]{1,2,0:T(8,128)(2,1)S(1)}, u32[]{:S(2)}, u32[]{:S(2)}) collective-permute-start(bf16[1,128,16]{1,2,0:T(8,128)(2,1)S(1)} %get-tuple-element.15), channel_id=1, source_target_pairs={{4,0},{8,4},{12,8},{16,12},{20,16},{24,20},{28,24},{32,28},{36,32}... | collective-permute-start | bytes 12296 | tf_op jit(solution)/shard_map/ppermute | solution.py:17
  193.2 3.8 %collective-permute-start.10 = (bf16[1,128,16]{1,2,0:T(8,128)(2,1)S(1)}, bf16[1,128,16]{1,2,0:T(8,128)(2,1)S(1)}, u32[]{:S(2)}, u32[]{:S(2)}) collective-permute-start(bf16[1,128,16]{1,2,0:T(8,128)(2,1)S(1)} %get-tuple-element.14), channel_id=1, source_target_pairs={{0,4},{4,8},{8,12},{12,16},{16,20},{20,24},{24,28},{28,32},{32,36}... | collective-permute-start | bytes 12296 | tf_op jit(solution)/shard_map/ppermute | solution.py:16
  225.4 7.7 %copy-start.4 = (bf16[8192,16]{0,1:T(8,128)(2,1)S(1)}, bf16[8192,16]{0,1:T(8,128)(2,1)}, u32[]{:S(2)}) copy-start(bf16[8192,16]{0,1:T(8,128)(2,1)} %param.9) | copy-start | bytes 786436
  228.4 10.6 %collective-permute-start.12 = (bf16[64,128,16]{1,2,0:T(8,128)(2,1)S(1)}, bf16[64,128,16]{1,2,0:T(8,128)(2,1)S(1)}, u32[]{:S(2)}, u32[]{:S(2)}) collective-permute-start(bf16[64,128,16]{1,2,0:T(8,128)(2,1)S(1)} %copy_bitcast_fusion), channel_id=1, source_target_pairs={{0,4},{4,8},{8,12},{12,16},{16,20},{20,24},{24,28},{28,32},{32,36}... | collective-permute-start | bytes 786440 | tf_op jit(solution)/shard_map/ppermute | solution.py:16
  231.8 7.2 %collective-permute-start.13 = (bf16[64,128,16]{1,2,0:T(8,128)(2,1)S(1)}, bf16[64,128,16]{1,2,0:T(8,128)(2,1)S(1)}, u32[]{:S(2)}, u32[]{:S(2)}) collective-permute-start(bf16[64,128,16]{1,2,0:T(8,128)(2,1)S(1)} %copy_bitcast_fusion), channel_id=1, source_target_pairs={{4,0},{8,4},{12,8},{16,12},{20,16},{24,20},{28,24},{32,28},{36,32}... | collective-permute-start | bytes 786440 | tf_op jit(solution)/shard_map/ppermute | solution.py:17
  234.1 15.8 %all-to-all-start = ((bf16[4,8192,16]{1,2,0:T(8,128)(2,1)}), bf16[4,8192,16]{1,2,0:T(8,128)(2,1)}, u32[]{:S(2)}, u32[]{:S(2)}) async-start(bf16[4,8192,16]{1,2,0:T(8,128)(2,1)} %stack.2), calls=%async_computation | async-start | bytes 2097152 | tf_op jit(solution)/shard_map/all_to_all | solution.py:107
  245.8 135.5 %copy-start.3 = (f32[8192,16]{0,1:T(8,128)}, f32[8192,16]{0,1:T(8,128)S(1)}, u32[]{:S(2)}) copy-start(f32[8192,16]{0,1:T(8,128)S(1)} %fusion.7) | copy-start | bytes 1572868
